TPU v7x, 128 devices: a whole 4x4x4 slice. The times are simulated.
128 devices in a mesh: dp: 8 (over z_lo, y), sp: 16 (over x, z_hi, core).
Axes of the slice: x: 4, y: 4, z: 4 (z_hi: 2, z_lo: 2; z = z_hi * 2 + z_lo), core: 2. Of those that a mesh axis runs over, the one named last changes fastest.
Arguments:
- feats: bfloat16 [8, 32, 256, 128], P('dp', None, 'sp'), may hold values from -62 to 62
- conv_w: bfloat16 [1152, 256], replicated, may hold values from -0.1875 to 0.1875
- group_norm_gain: float32 [256], replicated, may hold values from 0.5 to 1.5
- group_norm_bias: float32 [256], replicated, may hold values from -3 to 3
- emb_w: bfloat16 [256, 3072], replicated, may hold values from -0.375 to 0.375
- time_w: bfloat16 [256, 9216], replicated, may hold values from -0.375 to 0.375
- up_w: bfloat16 [3072, 6144], P(None, 'sp'), may hold values from -0.109375 to 0.109375
- down_w: bfloat16 [6144, 3072], P('sp'), may hold values from -0.078125 to 0.078125
- steps: int32 [8], P('dp'), may hold values from 0 to 999
- cotangent: bfloat16 [8, 2048, 3072], P('dp', 'sp'), may hold values from -28 to 28
Outputs:
- grad_conv: float32 [1152, 256], replicated
- grad_up: float32 [3072, 6144], P('dp', 'sp')
- grad_down: float32 [6144, 3072], P('sp', 'dp')
All inputs are finite; a program needn't handle non-finite values.
Results may differ from a plain program's by a relative error of at most 0.012.
Values may be sent and summed in bfloat16 or wider, within the bound.
A program may use at most 192 MiB of HBM per device.

v0:
```python
import math
import jax
import jax.numpy as jnp
from jax import lax
from jax.sharding import Mesh
from jax.sharding import PartitionSpec as P

NORM_GROUPS = 32
SP = ("sp_0", "sp_1", "sp_2")
DP_SP = ("dp", "sp_0", "sp_1", "sp_2")


def from_behind(array, axis, by):
    length = lax.axis_size(axis)
    pairs = [(i, i + by) for i in range(length) if 0 <= i + by < length]
    return lax.ppermute(array, axis, pairs)


def copy_for_each(array, axis):
    length = lax.axis_size(axis)
    return lax.all_to_all(
        jnp.broadcast_to(array[None], (length, *array.shape)), axis, 0, 0, tiled=True
    )


def over_copies(array, axis):
    return copy_for_each(array, axis).sum(axis=0)


def in_one(arrays, axis):
    ends = [0]
    for a in arrays:
        ends.append(ends[-1] + a.size)
    subtotal = over_copies(jnp.concatenate([a.ravel() for a in arrays]), axis)
    return tuple((subtotal[b:e].reshape(a.shape) for a, b, e in zip(arrays, ends, ends[1:])))


def in_blocks(array, dim, length):
    before, after = (array.shape[:dim], array.shape[dim + 1 :])
    return jnp.moveaxis(array.reshape(*before, length, -1, *after), dim, 0)


def sum_by_chip(array, chips, core, dim):
    sizes = (lax.axis_size(chips), lax.axis_size(core))
    parts = in_blocks(array, dim, sizes[0] * sizes[1])
    inside = parts.shape[1:]
    parts = parts.reshape(*sizes, *inside).swapaxes(0, 1).reshape(-1, *inside)
    parts = lax.psum_scatter(parts, core, scatter_dimension=0, tiled=True)
    return lax.psum_scatter(parts, chips, scatter_dimension=0, tiled=True)[0]


def sum_packed(arrays, axis, dims):
    length = lax.axis_size(axis)
    parts = [in_blocks(a, dim, length) for a, dim in zip(arrays, dims)]
    lines = jnp.concatenate([b.reshape(length, -1) for b in parts], axis=1)
    rows = max(16, -(-lines.shape[1] // 1024) * 8)
    lines = jnp.pad(lines, ((0, 0), (0, rows * 128 - lines.shape[1]))).reshape(-1, 128)
    ravelled, at, finished = (lax.psum_scatter(lines, axis, tiled=True).reshape(-1), 0, [])
    for b in parts:
        part = b[0]
        finished.append(ravelled[at : at + part.size].reshape(part.shape))
        at += part.size
    return tuple(finished)


def gelu_pair(u):
    coef = math.sqrt(2.0 / math.pi)
    inner = coef * (u + 0.044715 * u * u * u)
    tangent = jnp.tanh(inner)
    value = 0.5 * u * (1.0 + tangent)
    slope = 0.5 * (1.0 + tangent) + 0.5 * u * (1.0 - tangent * tangent) * coef * (
        1.0 + 3.0 * 0.044715 * u * u
    )
    return (value, slope)


def silu_pair(value):
    sigma = jax.nn.sigmoid(value)
    return (value * sigma, sigma * (1.0 + value * (1.0 - sigma)))


def modulation(step_value, time_w):
    half = time_w.shape[0] // 2
    freqs = jnp.exp(-math.log(10000.0) * jnp.arange(half, dtype=jnp.float32) / half)
    angle = step_value.astype(jnp.float32) * freqs
    embed = jnp.concatenate([jnp.cos(angle), jnp.sin(angle)])
    mixed = jnp.dot(
        jax.nn.silu(embed).astype(jnp.bfloat16)[None, :], time_w, preferred_element_type=jnp.float32
    )[0]
    width = time_w.shape[1] // 3
    return (mixed[:width], mixed[width : 2 * width], mixed[2 * width :])


def make_patches(padded, rows, cols):
    pieces = []
    for row_tap in range(3):
        for col_tap in range(3):
            pieces.append(
                padded[row_tap : row_tap + 2 * rows : 2, col_tap : col_tap + 2 * cols : 2, :]
            )
    stacked = jnp.concatenate(pieces, axis=-1)
    return stacked.reshape(rows * cols, stacked.shape[-1])


def group_totals(first, second, groups):
    tokens, width = first.shape
    first_g = first.reshape(tokens, groups, width // groups)
    second_g = second.reshape(tokens, groups, width // groups)
    return (jnp.sum(first_g, axis=(0, 2)), jnp.sum(second_g, axis=(0, 2)))


def broadcast_groups(values, width):
    return jnp.repeat(values, width // values.shape[0])


def contract(left, right, left_dim, right_dim):
    return lax.dot_general(
        left, right, (((left_dim,), (right_dim,)), ((), ())), preferred_element_type=jnp.float32
    )


def on_device(
    feats, conv_w, group_norm_gain, group_norm_bias, emb_w, time_w, up_w, down_w, steps, cotangent
):
    devices_sp = lax.axis_size(SP)
    image = feats[0]
    rows_in, cols_in, _ = image.shape
    rows = rows_in // 2
    cols = cols_in // 2
    seq_rows = rows // devices_sp
    channel_count = conv_w.shape[1]
    rim = from_behind(image[:, cols_in - 1, :], SP, 1)
    widened = jnp.concatenate([rim[:, None, :], image], axis=1)
    padded = jnp.pad(widened, ((1, 0), (0, 0), (0, 0)))
    patches = make_patches(padded, rows, cols)
    normed_value = jnp.dot(patches, conv_w, preferred_element_type=jnp.float32)
    first, second = group_totals(normed_value, normed_value * normed_value, NORM_GROUPS)
    first, second = in_one((first, second), SP)
    group_count = normed_value.shape[0] * devices_sp * (channel_count // NORM_GROUPS)
    group_mean = first / group_count
    rstd = lax.rsqrt(second / group_count - group_mean * group_mean + 1e-05)
    channel_rstd = broadcast_groups(rstd, channel_count)
    centered_input = (normed_value - broadcast_groups(group_mean, channel_count)) * channel_rstd
    preactivation = centered_input * group_norm_gain + group_norm_bias
    act_val, silu_slope = silu_pair(preactivation)
    act_b = act_val.astype(jnp.bfloat16)
    shift, scale, gate = modulation(steps[0], time_w)
    cot_seq = cotangent[0]
    width = emb_w.shape[1]
    all_cot = lax.all_gather(cot_seq, SP, axis=0, tiled=True)
    all_act = lax.all_gather(act_b.reshape(rows, cols, channel_count), SP, axis=1, tiled=True)
    all_act = all_act.reshape(rows * cols * devices_sp, channel_count)
    emb_f = emb_w.astype(jnp.float32)
    emb_mean = jnp.mean(emb_f, axis=1, keepdims=True)
    gram = contract(emb_w, emb_w, 1, 1) - width * emb_mean * emb_mean.T
    gram_hi = gram.astype(jnp.bfloat16)
    gram_lo = (gram - gram_hi.astype(jnp.float32)).astype(jnp.bfloat16)
    emb_c = emb_f - emb_mean
    mixer = jnp.dot(
        (emb_c * (1.0 + scale)).astype(jnp.bfloat16), up_w, preferred_element_type=jnp.float32
    ).astype(jnp.bfloat16)
    shift_hi = shift.astype(jnp.bfloat16)
    shift_lo = (shift - shift_hi.astype(jnp.float32)).astype(jnp.bfloat16)
    offset = jnp.dot(jnp.stack([shift_hi, shift_lo]), up_w, preferred_element_type=jnp.float32).sum(
        axis=0
    )
    act_gram = jnp.dot(all_act, gram_hi, preferred_element_type=jnp.float32) + jnp.dot(
        all_act, gram_lo, preferred_element_type=jnp.float32
    )
    token_var = jnp.sum(all_act.astype(jnp.float32) * act_gram, axis=-1, keepdims=True) / width
    token_rstd = lax.rsqrt(token_var + 1e-06)
    moved = token_rstd * jnp.dot(all_act, mixer, preferred_element_type=jnp.float32)
    gelu_val, gelu_slope = gelu_pair(moved + offset)
    hid = gelu_val.astype(jnp.bfloat16)
    dhid = contract(all_cot, (down_w.astype(jnp.float32) * gate).astype(jnp.bfloat16), 1, 1)
    dupper = dhid * gelu_slope
    dupper_sum = jnp.sum(dupper, axis=0)
    dupper_r = (dupper * token_rstd).astype(jnp.bfloat16)
    cross = jnp.sum(dupper_r.astype(jnp.float32) * moved, axis=-1, keepdims=True)
    part = contract(dupper_r, mixer, 1, 1) - cross * token_rstd * act_gram / width
    dact = sum_by_chip(part.astype(jnp.bfloat16), ("sp_0", "sp_1"), "sp_2", 0).astype(jnp.float32)
    dact = dact + contract(cot_seq, emb_w, 1, 1)
    pair = contract(all_act, dupper_r, 0, 0).astype(jnp.bfloat16)
    grad_down_local = contract(hid, all_cot, 0, 0) * gate
    (grad_down,) = sum_packed((grad_down_local.astype(jnp.bfloat16),), "dp", (1,))
    grad_down = grad_down.astype(jnp.float32)
    all_pair = lax.all_gather(pair, "dp", axis=0, tiled=True)
    side = lax.all_gather(jnp.concatenate([1.0 + scale, shift, dupper_sum]), "dp", axis=0)
    here = lax.axis_index("dp")
    block = width // lax.axis_size("dp")
    emb_here = lax.dynamic_slice_in_dim(emb_c, here * block, block, 1)
    scale_here = lax.dynamic_slice_in_dim(side[:, :width], here * block, block, 1)
    shift_here = lax.dynamic_slice_in_dim(side[:, width : 2 * width], here * block, block, 1)
    left = (emb_here[None] * scale_here[:, None, :]).astype(jnp.bfloat16)
    grad_up = contract(left.reshape(-1, block), all_pair, 0, 0) + lax.dot_general(
        shift_here, side[:, 2 * width :], (((0,), (0,)), ((), ())), precision=lax.Precision.HIGHEST
    )
    back_tiles = lax.all_to_all(
        dact.reshape(seq_rows, cols * devices_sp, channel_count).astype(jnp.bfloat16),
        SP,
        split_axis=1,
        concat_axis=0,
        tiled=True,
    ).astype(jnp.float32)
    dact_tile = back_tiles.reshape(rows * cols, channel_count)
    input_gradient = dact_tile * silu_slope * group_norm_gain
    backward_first, backward_second = group_totals(
        input_gradient, input_gradient * centered_input, NORM_GROUPS
    )
    backward_first, backward_second = in_one((backward_first, backward_second), SP)
    normed_gradient = (
        channel_rstd
        * (
            input_gradient
            - broadcast_groups(backward_first / group_count, channel_count)
            - centered_input * broadcast_groups(backward_second / group_count, channel_count)
        )
    ).astype(jnp.bfloat16)
    conv_local = contract(patches, normed_gradient, 0, 0)
    grad_conv = lax.psum(conv_local, DP_SP)
    return (grad_conv, grad_up, grad_down)


def solution(mesh):
    finer = Mesh(mesh.devices.reshape(mesh.shape["dp"], 4, 2, 2), ("dp", "sp_0", "sp_1", "sp_2"))
    in_specs = (
        P("dp", None, SP, None),
        P(),
        P(),
        P(),
        P(),
        P(),
        P(None, SP),
        P(SP, None),
        P("dp"),
        P("dp", SP, None),
    )
    out_specs = (P(), P("dp", SP), P(SP, "dp"))
    return jax.shard_map(
        on_device, mesh=finer, in_specs=in_specs, out_specs=out_specs, check_vma=False
    )
```

profile of v0, /device:TPU:1, one launch (start us, length us, event | category | flops | bytes accessed | tf_op | source)
XLA Modules:
  0.0 519.2 jit_solution(354148787067696151)
XLA Ops:
  8.3 6.9 %collective-permute-start = (bf16[32,128]{1,0:T(8,128)(2,1)S(1)}, bf16[32,128]{1,0:T(8,128)(2,1)S(1)}, u32[]{:S(2)}, u32[]{:S(2)}) collective-permute-start(bf16[32,128]{1,0:T(8,128)(2,1)S(1)} %slice_bitcast_fusion), channel_id=1, source_target_pairs={{0,1},{1,2},{2,3},{3,4},{4,5},{5,6},{6,7},{7,8},{8,9},{9,10},{10,1... | collective-permute-start | bytes 24584 | tf_op jit(solution)/shard_map/ppermute | solution.py:16
  21.2 14.7 %all_to_all.21 = f32[16,1,64]{2,1,0:T(1,128)S(1)} all-to-all(f32[16,1,64]{2,1,0:T(1,128)S(1)} %broadcast_in_dim.15), channel_id=1, replica_groups=mesh['dp'=8,'sp_0'=4,'sp_1'=2,'sp_2'=2] {'sp_0','sp_1','sp_2'}, dimensions={0} | all-to-all | bytes 8192 | tf_op jit(solution)/shard_map/all_to_all | solution.py:21
  39.4 3.1 fusion.65
  47.5 33.8 %all-gather.7.cloned.1.call-done = bf16[16,128,256]{2,1,0:T(8,128)(2,1)} async-done(((bf16[16,8,256]{2,1,0:T(8,128)(2,1)}), bf16[16,128,256]{2,1,0:T(8,128)(2,1)}) %all-gather.7.cloned.1.call-update) | async-done | bytes 1048592 | tf_op jit(solution)/shard_map/all_gather | solution.py:151
  84.9 2.3 convolution_multiply_fusion
  87.2 86.0 %all-gather.11.cloned.1.call-done = bf16[1,2048,3072]{2,1,0:T(8,128)(2,1)} async-done(((bf16[1,128,3072]{2,1,0:T(8,128)(2,1)}), bf16[1,2048,3072]{2,1,0:T(8,128)(2,1)}) %all-gather.11.cloned.1.call-update) | async-done | bytes 12582928 | tf_op jit(solution)/shard_map/all_gather | solution.py:150
  173.2 12.1 %multiply_reduce_fusion = (f32[2048]{0:T(1024)S(1)}, bf16[2048,384]{0,1:T(8,128)(2,1)S(1)}, f32[384]{0:T(512)}) fusion(f32[2048,384]{0,1:T(8,128)} %convolution_multiply_fusion, f32[2048]{0:T(1024)S(1)} %add_rsqrt_fusion, f32[384]{0:T(512)} %convolution_reduce_fusion, bf16[1,2048,3072]{2,1,0:T(8,128)(2,1)} %all-gather.11.cloned.1.call-done, ...), kind=kOutput, calls=%fused_computation.18 | convolution fusion | flops 4855035392 | bytes 19692544 | tf_op jit(solution)/shard_map/dot_general | solution.py:117
  187.3 9.0 %reduce-scatter.4.cloned.1.call-done = bf16[8,128,256]{2,1,0:T(8,128)(2,1)} async-done(((bf16[16,128,256]{2,1,0:T(8,128)(2,1)}), bf16[8,128,256]{2,1,0:T(8,128)(2,1)}) %reduce-scatter.4.cloned.1.call-update) | async-done | bytes 524304 | tf_op jit(solution)/shard_map/reduce_scatter | solution.py:48
  196.4 2.9 convolution_convert_fusion
  199.5 10.9 %multiply_convert_fusion = bf16[384,3072]{1,0:T(8,128)(2,1)S(1)} fusion(bf16[1,2048,3072]{2,1,0:T(8,128)(2,1)} %all-gather.11.cloned.1.call-done, f32[3072]{0:T(1024)S(1)} %copy-done.18, f32[2048,384]{0,1:T(8,128)} %convolution_multiply_fusion, f32[384]{0:T(512)S(1)} %copy-done.24), kind=kOutput, calls=%fused_computation.6 | convolution fusion | flops 4842061824 | bytes 18101760 | tf_op jit(solution)/shard_map/dot_general | solution.py:117
  212.1 5.0 reshape.113
  220.0 23.3 %all-gather.2 = f32[8,1,6528]{2,1,0:T(1,128)S(1)} all-gather(f32[1,1,6528]{2,1,0:T(1,128)S(1)} %reshape.119), channel_id=3, replica_groups=mesh['dp'=8,'sp_0'=4,'sp_1'=2,'sp_2'=2] {'dp'}, dimensions={0}, use_global_device_ids=true | all-gather | bytes 235008 | tf_op jit(solution)/shard_map/all_gather | solution.py:188
  243.2 26.6 %reduce-scatter.6.cloned.1.call-done = bf16[1,128,256]{2,1,0:T(8,128)(2,1)} async-done(((bf16[8,128,256]{2,1,0:T(8,128)(2,1)}), bf16[1,128,256]{2,1,0:T(8,128)(2,1)}) %reduce-scatter.6.cloned.1.call-update) | async-done | bytes 65552 | tf_op jit(solution)/shard_map/reduce_scatter | solution.py:49
  269.9 2.1 fusion.25
  274.3 7.2 %all-to-all-start.1 = ((bf16[16,2,1024]{2,1,0:T(2,128)(2,1)}), bf16[16,2,1024]{2,1,0:T(2,128)(2,1)S(1)}, u32[]{:S(2)}, u32[]{:S(2)}) async-start(bf16[16,2,1024]{2,1,0:T(2,128)(2,1)} %reshape.124), calls=%async_computation.3 | async-start | bytes 131072 | tf_op jit(solution)/shard_map/all_to_all | solution.py:198
  282.1 7.1 %all-to-all-done.1 = bf16[16,2,1024]{2,1,0:T(2,128)(2,1)S(1)} async-done(((bf16[16,2,1024]{2,1,0:T(2,128)(2,1)}), bf16[16,2,1024]{2,1,0:T(2,128)(2,1)S(1)}, u32[]{:S(2)}, u32[]{:S(2)}) %all-to-all-start.1) | async-done | bytes 65568 | tf_op jit(solution)/shard_map/all_to_all | solution.py:198
  290.5 3.7 all-to-all-start.2
  294.3 6.9 %all-to-all-done.2 = f32[16,1,64]{2,1,0:T(1,128)S(1)} async-done(((f32[16,1,64]{2,1,0:T(1,128)}), f32[16,1,64]{2,1,0:T(1,128)S(1)}, u32[]{:S(2)}, u32[]{:S(2)}) %all-to-all-start.2) | async-done | bytes 4128 | tf_op jit(solution)/shard_map/all_to_all | solution.py:21
  301.6 2.3 fusion.29
  307.6 3.7 convolution_add_fusion.1
  311.3 41.8 %reduce-scatter.8.cloned.1.call-done = bf16[1152,128]{1,0:T(8,128)(2,1)} async-done(((bf16[9216,128]{1,0:T(8,128)(2,1)}), bf16[1152,128]{1,0:T(8,128)(2,1)}) %reduce-scatter.8.cloned.1.call-update) | async-done | bytes 294928 | tf_op jit(solution)/shard_map/reduce_scatter | solution.py:58
  353.1 1.9 reshape.116
  355.0 155.0 %all-reduce.3.cloned.1.call-done = f32[1152,256]{1,0:T(8,128)} async-done(((f32[1152,256]{1,0:T(8,128)}), f32[1152,256]{1,0:T(8,128)}) %all-reduce.3.cloned.1.call-update) | async-done | bytes 1179664 | tf_op jit(solution)/shard_map/psum | solution.py:220
  510.0 2.4 copy.81
  (146 shorter events, 33.2 us)
Async XLA Ops:
  7.2 36.3 %copy-start = (bf16[3072,384]{1,0:T(8,128)(2,1)S(1)}, bf16[3072,384]{1,0:T(8,128)(2,1)}, u32[]{:S(2)}) copy-start(bf16[3072,384]{1,0:T(8,128)(2,1)} %param.16) | copy-start | bytes 7077892
  7.2 74.1 %all-gather.7.cloned.1.call-start = ((), (), s32[]{:S(2)}) async-start(), calls=%async_computation.6 | async-start | bytes 1114112 | tf_op jit(solution)/shard_map/all_gather | solution.py:151
  8.3 7.7 %collective-permute-start = (bf16[32,128]{1,0:T(8,128)(2,1)S(1)}, bf16[32,128]{1,0:T(8,128)(2,1)S(1)}, u32[]{:S(2)}, u32[]{:S(2)}) collective-permute-start(bf16[32,128]{1,0:T(8,128)(2,1)S(1)} %slice_bitcast_fusion), channel_id=1, source_target_pairs={{0,1},{1,2},{2,3},{3,4},{4,5},{5,6},{6,7},{7,8},{8,9},{9,10},{10,1... | collective-permute-start | bytes 24584 | tf_op jit(solution)/shard_map/ppermute | solution.py:16
  36.2 7.2 %copy-start.14 = (f32[256]{0:T(256)}, f32[256]{0:T(256)S(1)}, u32[]{:S(2)}) copy-start(f32[256]{0:T(256)S(1)} %mul.219) | copy-start | bytes 3076
  36.3 7.1 %copy-start.16 = (f32[256]{0:T(256)}, f32[256]{0:T(256)S(1)}, u32[]{:S(2)}) copy-start(f32[256]{0:T(256)S(1)} %sub.53) | copy-start | bytes 3076
  37.7 135.5 %all-gather.11.cloned.1.call-start = ((), (), s32[]{:S(2)}) async-start(), calls=%async_computation.12 | async-start | bytes 13369344 | tf_op jit(solution)/shard_map/all_gather | solution.py:150
  38.5 157.8 %reduce-scatter.4.cloned.1.call-start = ((), (), s32[]{:S(2)}) async-start(), calls=%async_computation.7 | async-start | bytes 1572864 | tf_op jit(solution)/shard_map/reduce_scatter | solution.py:48
  173.2 12.1 %copy-start.3 = (f32[2048,256]{1,0:T(8,128)S(1)}, f32[2048,256]{1,0:T(8,128)}, u32[]{:S(2)}) copy-start(f32[2048,256]{1,0:T(8,128)} %get-tuple-element.24) | copy-start | bytes 6291460
  173.2 12.1 %copy-start.10 = (bf16[256,384]{1,0:T(8,128)(2,1)S(1)}, bf16[256,384]{1,0:T(8,128)(2,1)}, u32[]{:S(2)}) copy-start(bf16[256,384]{1,0:T(8,128)(2,1)} %fusion.23) | copy-start | bytes 589828
  186.2 13.3 %copy-start.18 = (f32[3072]{0:T(1024)S(1)}, f32[3072]{0:T(1024)}, u32[]{:S(2)}) copy-start(f32[3072]{0:T(1024)} %get-tuple-element.17) | copy-start | bytes 36868
  186.2 13.3 %copy-start.24 = (f32[384]{0:T(512)S(1)}, f32[384]{0:T(512)}, u32[]{:S(2)}) copy-start(f32[384]{0:T(512)} %convolution_reduce_fusion) | copy-start | bytes 4612
  187.3 82.6 %reduce-scatter.6.cloned.1.call-start = ((), (), s32[]{:S(2)}) async-start(), calls=%async_computation.8 | async-start | bytes 589824 | tf_op jit(solution)/shard_map/reduce_scatter | solution.py:49
  196.3 111.3 %all-gather.9.cloned.1.call-start = ((), (), s32[]{:S(2)}) async-start(), calls=%async_computation.10 | async-start | bytes 1769472 | tf_op jit(solution)/shard_map/all_gather | solution.py:187
  199.3 153.8 %reduce-scatter.8.cloned.1.call-start = ((), (), s32[]{:S(2)}) async-start(), calls=%async_computation.11 | async-start | bytes 2654208 | tf_op jit(solution)/shard_map/reduce_scatter | solution.py:58
  212.1 5.1 copy-start.22
  217.2 52.7 %copy-start.4 = (bf16[1,128,3072]{2,1,0:T(8,128)(2,1)S(1)}, bf16[1,128,3072]{2,1,0:T(8,128)(2,1)}, u32[]{:S(2)}) copy-start(bf16[1,128,3072]{2,1,0:T(8,128)(2,1)} %param.19) | copy-start | bytes 2359300
  219.1 70.1 %copy-start.15 = (f32[256]{0:T(256)S(1)}, f32[256]{0:T(256)}, u32[]{:S(2)}) copy-start(f32[256]{0:T(256)} %copy-done.14) | copy-start | bytes 3076
  219.1 70.1 %copy-start.17 = (f32[256]{0:T(256)S(1)}, f32[256]{0:T(256)}, u32[]{:S(2)}) copy-start(f32[256]{0:T(256)} %copy-done.16) | copy-start | bytes 3076
  219.1 70.1 %copy-start.19 = (f32[256]{0:T(256)S(1)}, f32[256]{0:T(256)}, u32[]{:S(2)}) copy-start(f32[256]{0:T(256)} %param.13) | copy-start | bytes 3076
  219.1 70.1 %copy-start.20 = (f32[256]{0:T(256)S(1)}, f32[256]{0:T(256)}, u32[]{:S(2)}) copy-start(f32[256]{0:T(256)} %param.12) | copy-start | bytes 3076
  272.0 32.0 %copy-start.6 = (f32[256,384]{1,0:T(8,128)S(1)}, f32[256,384]{1,0:T(8,128)}, u32[]{:S(2)}) copy-start(f32[256,384]{1,0:T(8,128)} %constant_dynamic-slice_fusion.1) | copy-start | bytes 1179652
  274.3 14.9 %all-to-all-start.1 = ((bf16[16,2,1024]{2,1,0:T(2,128)(2,1)}), bf16[16,2,1024]{2,1,0:T(2,128)(2,1)S(1)}, u32[]{:S(2)}, u32[]{:S(2)}) async-start(bf16[16,2,1024]{2,1,0:T(2,128)(2,1)} %reshape.124), calls=%async_computation.3 | async-start | bytes 131072 | tf_op jit(solution)/shard_map/all_to_all | solution.py:198
  290.5 10.7 %all-to-all-start.2 = ((f32[16,1,64]{2,1,0:T(1,128)}), f32[16,1,64]{2,1,0:T(1,128)S(1)}, u32[]{:S(2)}, u32[]{:S(2)}) async-start(f32[16,1,64]{2,1,0:T(1,128)} %broadcast_in_dim.18), calls=%async_computation.4 | async-start | bytes 16384 | tf_op jit(solution)/shard_map/all_to_all | solution.py:21
  294.2 215.8 %all-reduce.3.cloned.1.call-start = ((), (), s32[]{:S(2)}) async-start(), calls=%async_computation.9 | async-start | bytes 2359296 | tf_op jit(solution)/shard_map/psum | solution.py:220
  (11 other events, 27.7 us)
Sparse Core Ops, SparseCore 0:
  37.8 43.3 all-gather.6
  83.6 89.5 all-gather.10
  187.4 8.8 reduce-scatter.3
  200.2 69.6 reduce-scatter.5
  271.4 36.1 all-gather.8
  309.9 43.1 reduce-scatter.7
  358.4 151.5 all-reduce.2
where the time goes:
time: 520 us; the launch traced here: 519 us
  waiting for transfers between devices  368 us (71%)
  matrix products  50.6 us (10%)
  blocking collectives  38 us (7%)
  local copies, waits for them, and re-layouts  20.8 us (4%)
  starting transfers between devices  18.2 us (4%)
  between operations  15.5 us (3%)
  other arithmetic  7.73 us (1%)
    psum x1, waiting for transfers between devices, on_device(): grad_conv = lax.psum(conv_local, DP_SP)  155 us
    all_gather x1, waiting for transfers between devices, on_device(): all_cot = lax.all_gather(cot_seq, SP, axis=0, tiled=True)  86 us
    reduce_scatter x1, waiting for transfers between devices, sum_packed(): lax.psum_scatter(lines, axis, tiled=True).reshape(-1)  41.8 us
    dot_general x8, matrix products, contract(): lax.dot_general(left, right, (((left_dim,), (right_dim,)), ((), ())), pre...  36.1 us
    all_gather x1, waiting for transfers between devices, on_device(): lax.all_gather(act_b.reshape(rows, cols, channel_count), SP, axis=1, tile...  33.8 us
    reduce_scatter x1, waiting for transfers between devices, sum_by_chip(): return lax.psum_scatter(parts, chips, scatter_dimension=0, tiled=True)[0]  26.6 us
    all_gather x1, blocking collectives, on_device(): lax.all_gather(jnp.concatenate([1.0 + scale, shift, dupper_sum]), 'dp', a...  23.3 us
    all_to_all x1, blocking collectives, copy_for_each(): lax.all_to_all(jnp.broadcast_to(array[None], (length, *array.shape)), axi...  14.7 us
  transfers between devices with their start and end apart: 10, of which 10 were waited for; matrix products, arithmetic and copies ran while one was open for 11% of the time, Pallas kernels for 0%

commit v1 on v0

--- a/solution.py
+++ b/solution.py
@@ -217,7 +217,8 @@
         )
     ).astype(jnp.bfloat16)
     conv_local = contract(patches, normed_gradient, 0, 0)
-    grad_conv = lax.psum(conv_local, DP_SP)
+    shards = lax.all_gather(conv_local, DP_SP, axis=0, tiled=False)
+    grad_conv = shards.sum(axis=0)
     return (grad_conv, grad_up, grad_down)
 
 

time: 520 us -> 1220 us (2.35)
  waiting for transfers between devices: 368 us -> 1020 us
  other arithmetic: 7.73 us -> 54.2 us
  blocking collectives: 38 us -> 62.2 us
    all_gather x0 -> x1, waiting for transfers between devices: none -> 815 us  [on_device(): shards = lax.all_gather(conv_local, DP_SP, axis=0, tiled=False)]
    psum x1 -> x0, waiting for transfers between devices: 155 us -> none  [on_device(): grad_conv = lax.psum(conv_local, DP_SP)]
    reduce_sum x0 -> x1, other arithmetic: none -> 46.5 us  [on_device(): grad_conv = shards.sum(axis=0)]
    reduce_scatter x1, waiting for transfers between devices: 26.6 us -> 52.7 us  [sum_by_chip(): return lax.psum_scatter(parts, chips, scatter_dimension=0, tiled=True)[0]]
    reduce_scatter x1, waiting for transfers between devices: 41.8 us -> 21.3 us  [sum_packed(): lax.psum_scatter(lines, axis, tiled=True).reshape(-1)]
    all_to_all x0 -> x1, blocking collectives: none -> 14.4 us  [on_device(): lax.all_to_all(dact.reshape(seq_rows, cols * devices_sp, channel_count).a...]
    all_to_all x2 -> x0, waiting for transfers between devices: 14 us -> none  [the longest x1 7.08 us: on_device(): lax.all_to_all(dact.reshape(seq_rows, cols * devices_sp, channel_count).a...]
    all_to_all x1 -> x2, blocking collectives: 14.7 us -> 24.6 us  [copy_for_each(): lax.all_to_all(jnp.broadcast_to(array[None], (length, *array.shape)), axi...]
  transfers between devices with their start and end apart: 10 -> 8, of which waited for: 10 -> 7; matrix products, arithmetic and copies ran while one was open for 11% -> 4% of each run, Pallas kernels for 0% -> 0%
where the time goes in v1:
time: 1220 us
  waiting for transfers between devices  1020 us (84%)
  blocking collectives  62.2 us (5%)
  other arithmetic  54.2 us (4%)
  matrix products  49.9 us (4%)
  local copies, waits for them, and re-layouts  15.8 us (1%)
  between operations  15.5 us (1%)
    all_gather x1, waiting for transfers between devices, on_device(): shards = lax.all_gather(conv_local, DP_SP, axis=0, tiled=False)  815 us
    all_gather x1, waiting for transfers between devices, on_device(): all_cot = lax.all_gather(cot_seq, SP, axis=0, tiled=True)  86 us
    reduce_scatter x1, waiting for transfers between devices, sum_by_chip(): return lax.psum_scatter(parts, chips, scatter_dimension=0, tiled=True)[0]  52.7 us
    reduce_sum x1, other arithmetic, on_device(): grad_conv = shards.sum(axis=0)  46.5 us
    dot_general x8, matrix products, contract(): lax.dot_general(left, right, (((left_dim,), (right_dim,)), ((), ())), pre...  36.1 us
    all_gather x1, waiting for transfers between devices, on_device(): lax.all_gather(act_b.reshape(rows, cols, channel_count), SP, axis=1, tile...  33.7 us
    all_to_all x2, blocking collectives, copy_for_each(): lax.all_to_all(jnp.broadcast_to(array[None], (length, *array.shape)), axi...  24.6 us
  transfers between devices with their start and end apart: 8, of which 7 were waited for; matrix products, arithmetic and copies ran while one was open for 4% of the time, Pallas kernels for 0%

profile of v1, /device:TPU:1, one launch (start us, length us, event | category | flops | bytes accessed | tf_op | source)
XLA Modules:
  0.0 1223.8 jit_solution(1751396892546272477)
XLA Ops:
  8.3 6.9 collective-permute-start
  21.2 14.7 %all_to_all.21 = f32[16,1,64]{2,1,0:T(1,128)S(1)} all-to-all(f32[16,1,64]{2,1,0:T(1,128)S(1)} %broadcast_in_dim.15), channel_id=1, replica_groups=mesh['dp'=8,'sp_0'=4,'sp_1'=2,'sp_2'=2] {'sp_0','sp_1','sp_2'}, dimensions={0} | all-to-all | bytes 8192 | tf_op jit(solution)/shard_map/all_to_all | solution.py:21
  39.4 3.1 fusion.65
  47.5 33.7 %all-gather.9.cloned.1.call-done = bf16[16,128,256]{2,1,0:T(8,128)(2,1)} async-done(((bf16[16,8,256]{2,1,0:T(8,128)(2,1)}), bf16[16,128,256]{2,1,0:T(8,128)(2,1)}) %all-gather.9.cloned.1.call-update) | async-done | bytes 1048592 | tf_op jit(solution)/shard_map/all_gather | solution.py:151
  83.1 1.8 multiply_reduce_fusion.1
  84.9 2.3 convolution_multiply_fusion
  87.2 86.0 %all-gather.13.cloned.1.call-done = bf16[1,2048,3072]{2,1,0:T(8,128)(2,1)} async-done(((bf16[1,128,3072]{2,1,0:T(8,128)(2,1)}), bf16[1,2048,3072]{2,1,0:T(8,128)(2,1)}) %all-gather.13.cloned.1.call-update) | async-done | bytes 12582928 | tf_op jit(solution)/shard_map/all_gather | solution.py:150
  173.2 12.1 multiply_reduce_fusion
  187.3 9.0 reduce-scatter.4.cloned.1.call-done
  196.4 2.8 convolution_convert_fusion
  199.5 10.9 multiply_convert_fusion
  212.1 5.0 reshape.113
  217.3 52.7 %reduce-scatter.6.cloned.1.call-done = bf16[1,128,256]{2,1,0:T(8,128)(2,1)} async-done(((bf16[8,128,256]{2,1,0:T(8,128)(2,1)}), bf16[1,128,256]{2,1,0:T(8,128)(2,1)}) %reduce-scatter.6.cloned.1.call-update) | async-done | bytes 65552 | tf_op jit(solution)/shard_map/reduce_scatter | solution.py:49
  269.9 2.1 fusion.25
  273.7 14.4 %all_to_all.22 = bf16[16,2,1024]{2,1,0:T(2,128)(2,1)S(1)} all-to-all(bf16[16,2,1024]{2,1,0:T(2,128)(2,1)S(1)} %reshape.125), channel_id=1, replica_groups=mesh['dp'=8,'sp_0'=4,'sp_1'=2,'sp_2'=2] {'sp_0','sp_1','sp_2'}, dimensions={0} | all-to-all | bytes 131072 | tf_op jit(solution)/shard_map/all_to_all | solution.py:198
  288.8 9.9 all_to_all.23
  299.1 2.3 fusion.29
  301.5 1.8 convert_subtract_fusion
  303.4 23.2 %all-gather.3 = f32[8,1,6528]{2,1,0:T(1,128)S(1)} all-gather(f32[1,1,6528]{2,1,0:T(1,128)S(1)} %reshape.120), channel_id=4, replica_groups=mesh['dp'=8,'sp_0'=4,'sp_1'=2,'sp_2'=2] {'dp'}, dimensions={0}, use_global_device_ids=true | all-gather | bytes 235008 | tf_op jit(solution)/shard_map/all_gather | solution.py:188
  328.9 3.7 convolution_add_fusion.1
  332.6 21.3 %reduce-scatter.8.cloned.1.call-done = bf16[1152,128]{1,0:T(8,128)(2,1)} async-done(((bf16[9216,128]{1,0:T(8,128)(2,1)}), bf16[1152,128]{1,0:T(8,128)(2,1)}) %reduce-scatter.8.cloned.1.call-update) | async-done | bytes 294928 | tf_op jit(solution)/shard_map/reduce_scatter | solution.py:58
  353.9 1.9 reshape.116
  355.8 814.5 %all-gather.15.cloned.1.call-done = f32[147456,256]{1,0:T(8,128)} async-done(((f32[1152,256]{1,0:T(8,128)}), f32[147456,256]{1,0:T(8,128)}) %all-gather.15.cloned.1.call-update) | async-done | bytes 150994960 | tf_op jit(solution)/shard_map/all_gather | solution.py:220
  1170.4 46.5 %reduce_sum.154 = f32[1152,256]{1,0:T(8,128)} reduce(f32[128,1152,256]{2,1,0:T(8,128)} %bitcast.19, f32[]{:T(128)} %constant.18.clone.1), dimensions={0}, to_apply=%region_16.17 | reduce | flops 37453824 | bytes 152174592 | tf_op jit(solution)/shard_map/reduce_sum | solution.py:221
  (142 shorter events, 25.5 us)
Async XLA Ops:
  7.2 36.3 %copy-start = (bf16[3072,384]{1,0:T(8,128)(2,1)S(1)}, bf16[3072,384]{1,0:T(8,128)(2,1)}, u32[]{:S(2)}) copy-start(bf16[3072,384]{1,0:T(8,128)(2,1)} %param.16) | copy-start | bytes 7077892
  7.2 74.1 %all-gather.9.cloned.1.call-start = ((), (), s32[]{:S(2)}) async-start(), calls=%async_computation.6 | async-start | bytes 1114112 | tf_op jit(solution)/shard_map/all_gather | solution.py:151
  8.3 7.7 collective-permute-start
  36.2 7.2 copy-start.13
  36.3 7.1 copy-start.15
  37.7 135.5 %all-gather.13.cloned.1.call-start = ((), (), s32[]{:S(2)}) async-start(), calls=%async_computation.11 | async-start | bytes 13369344 | tf_op jit(solution)/shard_map/all_gather | solution.py:150
  38.5 157.9 %reduce-scatter.4.cloned.1.call-start = ((), (), s32[]{:S(2)}) async-start(), calls=%async_computation.7 | async-start | bytes 1572864 | tf_op jit(solution)/shard_map/reduce_scatter | solution.py:48
  38.5 4.6 copy-start.2
  43.1 2.7 copy-start.11
  43.4 4.1 copy-start.20
  173.2 12.1 copy-start.3
  173.2 12.1 copy-start.9
  186.2 13.3 %copy-start.17 = (f32[3072]{0:T(1024)S(1)}, f32[3072]{0:T(1024)}, u32[]{:S(2)}) copy-start(f32[3072]{0:T(1024)} %get-tuple-element.17) | copy-start | bytes 36868
  186.2 13.3 %copy-start.23 = (f32[384]{0:T(512)S(1)}, f32[384]{0:T(512)}, u32[]{:S(2)}) copy-start(f32[384]{0:T(512)} %convolution_reduce_fusion) | copy-start | bytes 4612
  187.3 82.7 %reduce-scatter.6.cloned.1.call-start = ((), (), s32[]{:S(2)}) async-start(), calls=%async_computation.8 | async-start | bytes 589824 | tf_op jit(solution)/shard_map/reduce_scatter | solution.py:49
  196.4 132.5 %all-gather.11.cloned.1.call-start = ((), (), s32[]{:S(2)}) async-start(), calls=%async_computation.9 | async-start | bytes 1769472 | tf_op jit(solution)/shard_map/all_gather | solution.py:187
  199.3 154.7 %reduce-scatter.8.cloned.1.call-start = ((), (), s32[]{:S(2)}) async-start(), calls=%async_computation.10 | async-start | bytes 2654208 | tf_op jit(solution)/shard_map/reduce_scatter | solution.py:58
  212.1 57.8 %copy-start.4 = (bf16[1,128,3072]{2,1,0:T(8,128)(2,1)S(1)}, bf16[1,128,3072]{2,1,0:T(8,128)(2,1)}, u32[]{:S(2)}) copy-start(bf16[1,128,3072]{2,1,0:T(8,128)(2,1)} %param.19) | copy-start | bytes 2359300
  217.2 71.0 %copy-start.14 = (f32[256]{0:T(256)S(1)}, f32[256]{0:T(256)}, u32[]{:S(2)}) copy-start(f32[256]{0:T(256)} %copy-done.13) | copy-start | bytes 3076
  217.2 71.0 %copy-start.16 = (f32[256]{0:T(256)S(1)}, f32[256]{0:T(256)}, u32[]{:S(2)}) copy-start(f32[256]{0:T(256)} %copy-done.15) | copy-start | bytes 3076
  217.2 71.0 %copy-start.18 = (f32[256]{0:T(256)S(1)}, f32[256]{0:T(256)}, u32[]{:S(2)}) copy-start(f32[256]{0:T(256)} %param.13) | copy-start | bytes 3076
  217.2 71.0 %copy-start.19 = (f32[256]{0:T(256)S(1)}, f32[256]{0:T(256)}, u32[]{:S(2)}) copy-start(f32[256]{0:T(256)} %param.12) | copy-start | bytes 3076
  217.2 84.3 %copy-start.21 = (f32[256]{0:T(256)S(1)}, f32[256]{0:T(256)}, u32[]{:S(2)}) copy-start(f32[256]{0:T(256)} %copy-done.20) | copy-start | bytes 3076
  217.2 953.2 %all-gather.15.cloned.1.call-start = ((), (), s32[]{:S(2)}) async-start(), calls=%async_computation.12 | async-start | bytes 152174592 | tf_op jit(solution)/shard_map/all_gather | solution.py:220
  (8 other events, 13.9 us)
Sparse Core Ops, SparseCore 0:
  37.8 43.3 all-gather.8
  83.6 89.5 all-gather.12
  187.4 8.8 reduce-scatter.3
  200.2 69.7 reduce-scatter.5
  272.0 36.1 all-gather.10
  310.5 43.4 reduce-scatter.7
  356.2 814.0 all-gather.14
